TPU v7x, 32 devices: a whole 2x2x4 slice. The times are simulated.
32 devices in a mesh: dp: 8 (over z, x), mp: 4 (over y, core).
Axes of the slice: x: 2, y: 2, z: 4, core: 2. Of those that a mesh axis runs over, the one named last changes fastest.
Arguments:
- features: bfloat16 [8192, 1024], P('dp'), may hold values from -6 to 6
- out_grads: bfloat16 [8192, 4, 1024], P('dp', None, 'mp'), may hold values from -0.0625 to 0.0625
- norm_grads: float32 [8, 2048], P('dp'), may hold values from -2 to 2
- owners: int32 [5], replicated, may hold values from 0 to 7, as said below
- moment1: float32 [4, 1024, 1024], P(None, 'dp', 'mp'), may hold values from -6 to 6
- moment2: float32 [4, 1024, 1024], P(None, 'dp', 'mp'), may hold values from 0.1 to 10
- left_stats: float32 [4, 1024, 1024], P(None, 'dp', 'mp'), may hold values from -1024 to 1024, as said below
- right_stats: float32 [4, 1024, 1024], P(None, 'dp', 'mp'), may hold values from -1024 to 1024, as said below
- left_basis: float32 [4, 1024, 1024], P(None, 'dp', 'mp'), may hold values from -1 to 2
- right_basis: float32 [4, 1024, 1024], P(None, 'dp', 'mp'), may hold values from -1 to 2
- norm_m: float32 [2048], P('dp'), may hold values from -6 to 6
- norm_v: float32 [2048], P('dp'), may hold values from 0.1 to 10
Outputs:
- new_moment1: float32 [4, 1024, 1024], P(None, 'dp', 'mp')
- new_moment2: float32 [4, 1024, 1024], P(None, 'dp', 'mp')
- new_left_stats: float32 [4, 1024, 1024], P(None, 'dp', 'mp')
- new_right_stats: float32 [4, 1024, 1024], P(None, 'dp', 'mp')
- new_left_basis: float32 [4, 1024, 1024], P(None, 'dp', 'mp')
- new_right_basis: float32 [4, 1024, 1024], P(None, 'dp', 'mp')
- update_slots: bfloat16 [8, 1024, 1024], P('dp', None, 'mp')
- new_norm_m: float32 [2048], P('dp')
- new_norm_v: float32 [2048], P('dp')
- norm_slots: float32 [8, 2048], P('dp')
Inputs may be any that keep to these rules, and one draw needn't show every extreme that they name: `owners`: the first 4 entries are distinct, so a dp index owns at most one tile; the last entry may equal any of them. `left_stats`: each tile of statistics is symmetric. `right_stats`: each tile of statistics is symmetric.
All inputs are finite; a program needn't handle non-finite values.
Results may differ from a plain program's by a relative error of at most 0.0072.
Values may be sent and summed in bfloat16 or wider, within the bound.
A program may use at most 128 MiB of HBM per device.

v0:
```python
import jax
import jax.numpy as jnp
from jax import lax
from jax.sharding import PartitionSpec as P

FIX_ONE = 1.0 - 0.9**10
FIX_TWO = 1.0 - 0.95**10


def contract(left, right, left_dim, right_dim):
    return lax.dot_general(
        left, right, (((left_dim,), (right_dim,)), ((), ())), preferred_element_type=jnp.float32
    )


def normalize_columns(power):
    return (power * lax.rsqrt(jnp.sum(power * power, axis=0, keepdims=True) + 1e-06)).astype(
        jnp.bfloat16
    )


def shards(
    features,
    out_grads,
    norm_grads,
    owners,
    moment1,
    moment2,
    left_stats,
    right_stats,
    left_basis,
    right_basis,
    norm_m,
    norm_v,
):
    dp_count = lax.axis_size("dp")
    tile_count = moment1.shape[0]
    slab_rows = moment1.shape[1]
    width_mp = moment1.shape[2]
    full_tile = slab_rows * dp_count
    my_index = lax.axis_index("dp")
    col_start = lax.axis_index("mp") * width_mp
    tile_owner = owners[:tile_count]
    norm_owner = owners[tile_count]
    partial_value = jnp.einsum(
        "ti,tnc->nic", features, out_grads, preferred_element_type=jnp.float32
    )
    chooser = (tile_owner[None, :] == jnp.arange(dp_count, dtype=jnp.int32)[:, None]).astype(
        jnp.float32
    )
    matched = tile_owner == my_index
    owning = jnp.any(matched)
    state_list = [moment1, moment2, left_stats, right_stats]
    narrow_list = []
    norm_list = [norm_m, norm_v]
    narrow_list = [left_basis.astype(jnp.bfloat16), right_basis.astype(jnp.bfloat16)]
    summed, norm_total = lax.psum((partial_value, norm_grads[0]), "dp")
    tile_index = jnp.sum(jnp.where(matched, jnp.arange(tile_count, dtype=jnp.int32), 0))
    grad_mine = jnp.where(
        owning, lax.dynamic_index_in_dim(summed, tile_index, 0, keepdims=False), 0.0
    )
    grad_b = grad_mine.astype(jnp.bfloat16)
    home_stack = jnp.stack(state_list)
    outgoing = jnp.einsum("dn,knrc->kdrc", chooser, home_stack, precision=lax.Precision.HIGHEST)
    norm_stack = jnp.stack(norm_list)
    norm_mask = (jnp.arange(dp_count, dtype=jnp.int32) == norm_owner)[None, :, None]
    norm_out = jnp.where(norm_mask, norm_stack[:, None, :], 0.0)
    arrived, norm_arrived = (
        lax.all_to_all(outgoing, "dp", split_axis=1, concat_axis=1, tiled=True),
        lax.all_to_all(norm_out, "dp", split_axis=1, concat_axis=1, tiled=True),
    )
    arrived = arrived.reshape(arrived.shape[0], full_tile, width_mp)
    norm_arrived = norm_arrived.reshape(norm_arrived.shape[0], -1)
    narrow_stack = jnp.stack(narrow_list)
    narrow_out = jnp.einsum(
        "dn,knrc->kdrc",
        chooser.astype(jnp.bfloat16),
        narrow_stack,
        preferred_element_type=jnp.float32,
    ).astype(jnp.bfloat16)
    narrow_arrived = lax.all_to_all(narrow_out, "dp", split_axis=1, concat_axis=1, tiled=True)
    narrow_arrived = narrow_arrived.reshape(narrow_arrived.shape[0], full_tile, width_mp)
    left_local = narrow_arrived[0]
    right_local = narrow_arrived[1]
    grad_full, left_full, right_full = (
        lax.all_gather(grad_b, "mp", axis=1, tiled=True),
        lax.all_gather(left_local, "mp", axis=1, tiled=True),
        lax.all_gather(right_local, "mp", axis=1, tiled=True),
    )
    inner = jnp.dot(grad_full, right_local, preferred_element_type=jnp.float32).astype(jnp.bfloat16)
    rotated = contract(left_full, inner, 0, 0)
    new_one = 0.9 * arrived[0] + 0.1 * rotated
    new_two = 0.95 * arrived[1] + 0.05 * rotated * rotated
    direction = (new_one / FIX_ONE / (jnp.sqrt(new_two / FIX_TWO) + 1e-08)).astype(jnp.bfloat16)
    direction_full = lax.all_gather(direction, "mp", axis=1, tiled=True)
    right_rows = lax.dynamic_slice_in_dim(right_full, col_start, width_mp, 0)
    back = contract(direction_full, right_rows, 1, 1).astype(jnp.bfloat16)
    update = jnp.dot(left_full, back, preferred_element_type=jnp.float32)
    update_slot = jnp.where(owning, update, 0.0).astype(jnp.bfloat16)[None]
    grad_rows = lax.dynamic_slice_in_dim(grad_full, col_start, width_mp, 0)
    new_sl = 0.95 * arrived[2] + 0.05 * contract(grad_full, grad_rows, 1, 1)
    new_sr = 0.95 * arrived[3] + 0.05 * contract(grad_full, grad_b, 0, 0)
    stats_lfull, stats_rfull = (
        lax.all_gather(new_sl.astype(jnp.bfloat16), "mp", axis=1, tiled=True),
        lax.all_gather(new_sr.astype(jnp.bfloat16), "mp", axis=1, tiled=True),
    )
    iter_left = normalize_columns(
        jnp.dot(stats_lfull, left_local, preferred_element_type=jnp.float32)
    )
    iter_right = normalize_columns(
        jnp.dot(stats_rfull, right_local, preferred_element_type=jnp.float32)
    )
    left_iter_full, right_iter_full = (
        lax.all_gather(iter_left, "mp", axis=1, tiled=True),
        lax.all_gather(iter_right, "mp", axis=1, tiled=True),
    )
    gram_left = contract(left_iter_full, iter_left, 0, 0).astype(jnp.bfloat16)
    gram_right = contract(right_iter_full, iter_right, 0, 0).astype(jnp.bfloat16)
    new_bl = 1.5 * iter_left.astype(jnp.float32) - 0.5 * jnp.dot(
        left_iter_full, gram_left, preferred_element_type=jnp.float32
    )
    new_br = 1.5 * iter_right.astype(jnp.float32) - 0.5 * jnp.dot(
        right_iter_full, gram_right, preferred_element_type=jnp.float32
    )
    new_nm = 0.9 * norm_arrived[0] + 0.1 * norm_total
    new_nv = 0.95 * norm_arrived[1] + 0.05 * norm_total * norm_total
    norm_step = new_nm / FIX_ONE / (jnp.sqrt(new_nv / FIX_TWO) + 1e-08)
    norm_slot = jnp.where(my_index == norm_owner, norm_step, 0.0)[None]
    back_stack = jnp.stack([new_one, new_two, new_sl, new_sr, new_bl, new_br]).reshape(
        6, dp_count, slab_rows, width_mp
    )
    norm_back = jnp.stack([new_nm, new_nv]).reshape(2, dp_count, -1)
    returned, norm_returned = (
        lax.all_to_all(back_stack, "dp", split_axis=1, concat_axis=1, tiled=True),
        lax.all_to_all(norm_back, "dp", split_axis=1, concat_axis=1, tiled=True),
    )
    home_new = jnp.einsum("dn,kdrc->knrc", chooser, returned, precision=lax.Precision.HIGHEST)
    norm_new = lax.dynamic_index_in_dim(norm_returned, norm_owner, 1, keepdims=False)
    return (
        home_new[0],
        home_new[1],
        home_new[2],
        home_new[3],
        home_new[4],
        home_new[5],
        update_slot,
        norm_new[0],
        norm_new[1],
        norm_slot,
    )


def solution(mesh):
    in_specs = (
        P("dp", None),
        P("dp", None, "mp"),
        P("dp", None),
        P(),
        P(None, "dp", "mp"),
        P(None, "dp", "mp"),
        P(None, "dp", "mp"),
        P(None, "dp", "mp"),
        P(None, "dp", "mp"),
        P(None, "dp", "mp"),
        P("dp"),
        P("dp"),
    )
    out_specs = (
        P(None, "dp", "mp"),
        P(None, "dp", "mp"),
        P(None, "dp", "mp"),
        P(None, "dp", "mp"),
        P(None, "dp", "mp"),
        P(None, "dp", "mp"),
        P("dp", None, "mp"),
        P("dp"),
        P("dp"),
        P("dp", None),
    )
    return jax.shard_map(shards, mesh=mesh, in_specs=in_specs, out_specs=out_specs, check_vma=False)
```

profile of v0, /device:TPU:0, one launch (start us, length us, event | category | flops | bytes accessed | tf_op | source)
XLA Modules:
  0.0 588.9 jit_solution(5453987207880956669)
XLA Ops:
  7.2 1.4 fusion.68
  8.7 1.9 copy_bitcast_fusion.2
  10.6 0.7 copy_bitcast_fusion
  11.2 2.4 convolution_bitcast_fusion
  13.6 3.3 copy.70
  16.9 7.3 %all-to-all-start = ((f32[4,8,128,256]{3,2,0,1:T(8,128)}), f32[4,8,128,256]{3,2,0,1:T(8,128)}, u32[]{:S(2)}, u32[]{:S(2)}) async-start(f32[4,8,128,256]{3,2,0,1:T(8,128)} %copy.70), calls=%async_computation | async-start | bytes 8388608 | tf_op jit(solution)/shard_map/all_to_all | solution.py:69
  25.6 6.0 %convolution_bitcast_fusion.1 = f32[4,1024,256]{1,2,0:T(8,128)} fusion(bf16[1024,1024]{1,0:T(8,128)(2,1)S(1)} %copy-done, bf16[1024,4,256]{2,1,0:T(4,128)(2,1)} %param.13), kind=kOutput, calls=%fused_computation.3 | convolution fusion | flops 2147483648 | bytes 8388608 | tf_op jit(solution)/shard_map/ti,tnc->nic/dot_general | solution.py:45
  32.3 0.6 compare_reduce_fusion
  32.9 230.6 %all-reduce.2 = (bf16[4,1024,256]{1,2,0:T(8,128)(2,1)S(1)}, f32[2048]{0:T(1024)S(1)}) all-reduce(f32[4,1024,256]{1,2,0:T(8,128)} %convolution_bitcast_fusion.1, f32[2048]{0:T(1024)S(1)} %bitcast.173), channel_id=1, replica_groups=mesh['dp'=8,'mp'=4] {'dp'}, use_global_device_ids=true, to_apply=%region_1.0 | all-reduce | flops 1050624 | bytes 6307840 | tf_op jit(solution)/shard_map/psum | solution.py:57
  263.5 1.6 select_convert_fusion
  265.1 4.1 fusion.44
  269.2 21.9 %all-gather.24.cloned.1.call-done = bf16[1,1024,1024]{1,2,0:T(8,128)(2,1)} async-done(((bf16[1,1024,256]{1,2,0:T(8,128)(2,1)}), bf16[1,1024,1024]{1,2,0:T(8,128)(2,1)}) %all-gather.24.cloned.1.call-update) | async-done | bytes 2097168 | tf_op jit(solution)/shard_map/all_gather | solution.py:86
  291.1 3.6 fusion.76
  294.8 3.2 fusion.77
  298.0 0.2 all-gather.10.cloned.1.call-start
  298.3 1.1 convert_element_type.81
  299.4 0.4 copy_bitcast_fusion.4
  299.8 0.6 fusion.20
  300.3 0.2 copy.74
  300.6 31.4 %all_to_all.25 = bf16[2,8,128,256]{3,2,0,1:T(8,128)(2,1)S(1)} all-to-all(bf16[2,8,128,256]{3,2,0,1:T(8,128)(2,1)S(1)} %copy.74), channel_id=1, replica_groups=mesh['dp'=8,'mp'=4] {'dp'}, dimensions={1} | all-to-all | bytes 2097152 | tf_op jit(solution)/shard_map/all_to_all | solution.py:81
  332.0 0.9 fusion.73
  332.9 0.0 all-gather.14.cloned.1.call-start
  333.0 2.5 multiply_reduce_fusion.1
  335.5 0.9 multiply_convert_fusion.1
  336.4 6.2 %all-gather.16.cloned.1.call-done = bf16[1024,1024]{1,0:T(8,128)(2,1)} async-done(((bf16[1024,256]{1,0:T(8,128)(2,1)}), bf16[1024,1024]{1,0:T(8,128)(2,1)}) %all-gather.16.cloned.1.call-update) | async-done | bytes 2097168 | tf_op jit(solution)/shard_map/all_gather | solution.py:105
  342.7 2.3 multiply_reduce_fusion
  345.0 0.9 multiply_convert_fusion
  345.9 0.6 slice.77
  346.5 0.6 iota_compare_fusion.1
  347.2 0.7 broadcast_select_fusion
  347.9 5.5 all-to-all-start.3
  354.1 5.9 %all-to-all-done.3 = f32[2,8,256]{2,0,1:T(2,128)S(1)} async-done(((f32[2,8,256]{2,0,1:T(2,128)}), f32[2,8,256]{2,0,1:T(2,128)S(1)}, u32[]{:S(2)}, u32[]{:S(2)}) %all-to-all-start.3) | async-done | bytes 16416 | tf_op jit(solution)/shard_map/all_to_all | solution.py:70
  360.0 0.6 divide_select_fusion
  360.6 0.6 pad_maximum_fusion
  361.3 3.3 all-to-all-start.4
  364.6 2.9 all-gather.10.cloned.1.call-done
  367.5 6.6 %divide_convert_fusion = (bf16[1024,256]{1,0:T(8,128)(2,1)}, f32[1024,256]{1,0:T(8,128)S(1)}, f32[1024,256]{1,0:T(8,128)}) fusion(f32[1,8,128,256]{3,2,1,0:T(8,128)} %get-tuple-element.50, f32[1,8,128,256]{3,2,1,0:T(8,128)} %get-tuple-element.51, bf16[1024,1024]{1,0:T(8,128)(2,1)} %all-gather.10.cloned.1.call-done, bf16[1024,256]{1,0:T(8,128)(2,1)S(1)} %bitcast.159, ...), kind=kOutput, calls=%fused_computation.49 | convolution fusion | flops 1076625408 | bytes 9437184 | tf_op jit(solution)/shard_map/dot_general | solution.py:11
  374.1 2.4 constant_dynamic-update-slice_fusion.5
  376.5 1.2 constant_dynamic-update-slice_fusion.4
  377.7 1.1 constant_dynamic-update-slice_fusion.3
  378.8 1.1 constant_dynamic-update-slice_fusion.2
  379.9 12.4 %all-gather.14.cloned.1.call-done = bf16[1024,1024]{1,0:T(8,128)(2,1)} async-done(((bf16[1024,256]{1,0:T(8,128)(2,1)}), bf16[1024,1024]{1,0:T(8,128)(2,1)}) %all-gather.14.cloned.1.call-update) | async-done | bytes 2097168 | tf_op jit(solution)/shard_map/all_gather | solution.py:114
  392.3 4.5 fusion.34
  396.8 1.1 constant_dynamic-update-slice_fusion.1
  397.9 19.3 %all-gather.18.cloned.1.call-done = bf16[1024,1024]{1,0:T(8,128)(2,1)} async-done(((bf16[1024,256]{1,0:T(8,128)(2,1)}), bf16[1024,1024]{1,0:T(8,128)(2,1)}) %all-gather.18.cloned.1.call-update) | async-done | bytes 2097168 | tf_op jit(solution)/shard_map/all_gather | solution.py:115
  417.2 4.5 fusion.33
  421.6 1.1 constant_dynamic-update-slice_fusion
  422.7 5.6 all-to-all-start.2
  428.4 0.7 all-gather.22.cloned.1.call-update
  429.1 0.3 all-gather.20.cloned.1.call-start
  429.4 0.5 all-gather.20.cloned.1.call-update
  431.8 0.6 constant_dynamic-slice_fusion.1
  432.4 22.2 %all-gather.22.cloned.1.call-done = bf16[1024,1024]{1,0:T(8,128)(2,1)} async-done(((bf16[1024,256]{1,0:T(8,128)(2,1)}), bf16[1024,1024]{1,0:T(8,128)(2,1)}) %all-gather.22.cloned.1.call-update) | async-done | bytes 2097168 | tf_op jit(solution)/shard_map/all_gather | solution.py:88
  454.6 25.0 %all-gather.20.cloned.1.call-done = bf16[1024,1024]{1,0:T(8,128)(2,1)} async-done(((bf16[1024,256]{1,0:T(8,128)(2,1)}), bf16[1024,1024]{1,0:T(8,128)(2,1)}) %all-gather.20.cloned.1.call-update) | async-done | bytes 2097168 | tf_op jit(solution)/shard_map/all_gather | solution.py:95
  479.6 5.4 fusion.39
  485.0 82.0 %all-to-all-done.2 = f32[6,8,128,256]{3,2,0,1:T(8,128)} async-done(((f32[6,8,128,256]{3,2,0,1:T(8,128)}), f32[6,8,128,256]{3,2,0,1:T(8,128)}, u32[]{:S(2)}, u32[]{:S(2)}) %all-to-all-start.2) | async-done | bytes 6291488 | tf_op jit(solution)/shard_map/all_to_all | solution.py:134
  567.0 9.1 %fusion.17 = f32[6,4,128,256]{3,1,2,0:T(4,128)S(1)} fusion(f32[6,8,128,256]{3,2,0,1:T(8,128)} %all-to-all-done.2, s32[4]{0:T(128)S(1)} %get-tuple-element.65), kind=kOutput, calls=%fused_computation.19 | convolution fusion | flops 75497504 | bytes 9437200 | tf_op jit(solution)/shard_map/dn,kdrc->knrc/dot_general | solution.py:137
  576.1 0.5 slice_bitcast_fusion.4
  576.7 0.9 copy.93
  577.6 0.9 copy.92
  578.5 0.9 copy.91
  579.4 0.9 copy.90
  580.3 0.9 copy.89
  581.1 0.9 copy.88
  (49 shorter events, 0.5 us)
Async XLA Ops:
  7.2 18.4 %copy-start = (bf16[1024,1024]{1,0:T(8,128)(2,1)S(1)}, bf16[1024,1024]{1,0:T(8,128)(2,1)}, u32[]{:S(2)}) copy-start(bf16[1024,1024]{1,0:T(8,128)(2,1)} %param.12) | copy-start | bytes 6291460
  7.2 3.4 copy-start.8
  7.2 3.4 copy-start.9
  16.9 248.2 %all-to-all-start = ((f32[4,8,128,256]{3,2,0,1:T(8,128)}), f32[4,8,128,256]{3,2,0,1:T(8,128)}, u32[]{:S(2)}, u32[]{:S(2)}) async-start(f32[4,8,128,256]{3,2,0,1:T(8,128)} %copy.70), calls=%async_computation | async-start | bytes 8388608 | tf_op jit(solution)/shard_map/all_to_all | solution.py:69
  24.2 266.9 %all-gather.24.cloned.1.call-start = ((), (), s32[]{:S(2)}) async-start(), calls=%async_computation.12 | async-start | bytes 2621440 | tf_op jit(solution)/shard_map/all_gather | solution.py:86
  25.5 6.7 %copy-start.13 = (s32[5]{0:T(128)S(1)}, s32[5]{0:T(128)}, u32[]{:S(2)}) copy-start(s32[5]{0:T(128)} %param.15) | copy-start | bytes 64
  25.6 7.4 %copy-start.10 = (f32[1,2048]{1,0:T(1,128)S(1)}, f32[1,2048]{1,0:T(1,128)}, u32[]{:S(2)}) copy-start(f32[1,2048]{1,0:T(1,128)} %param.14) | copy-start | bytes 24580
  265.1 67.9 %all-gather.12.cloned.1.call-start = ((), (), s32[]{:S(2)}) async-start(), calls=%async_computation.6 | async-start | bytes 2621440 | tf_op jit(solution)/shard_map/all_gather | solution.py:104
  291.1 3.7 copy-start.2
  294.7 48.0 %all-gather.16.cloned.1.call-start = ((), (), s32[]{:S(2)}) async-start(), calls=%async_computation.8 | async-start | bytes 2621440 | tf_op jit(solution)/shard_map/all_gather | solution.py:105
  294.8 3.5 copy-start.7
  298.0 69.5 %all-gather.10.cloned.1.call-start = ((), (), s32[]{:S(2)}) async-start(), calls=%async_computation.5 | async-start | bytes 2621440 | tf_op jit(solution)/shard_map/all_gather | solution.py:87
  332.9 34.6 %copy-start.3 = (bf16[1,8,128,256]{3,2,0,1:T(8,128)(2,1)}, bf16[1,8,128,256]{3,2,0,1:T(8,128)(2,1)S(1)}, u32[]{:S(2)}) copy-start(bf16[1,8,128,256]{3,2,0,1:T(8,128)(2,1)S(1)} %get-tuple-element.58) | copy-start | bytes 1572868
  332.9 59.4 %all-gather.14.cloned.1.call-start = ((), (), s32[]{:S(2)}) async-start(), calls=%async_computation.7 | async-start | bytes 2621440 | tf_op jit(solution)/shard_map/all_gather | solution.py:114
  336.4 80.8 %all-gather.18.cloned.1.call-start = ((), (), s32[]{:S(2)}) async-start(), calls=%async_computation.9 | async-start | bytes 2621440 | tf_op jit(solution)/shard_map/all_gather | solution.py:115
  345.0 2.2 copy-start.11
  345.0 2.2 copy-start.12
  347.9 12.1 %all-to-all-start.3 = ((f32[2,8,256]{2,0,1:T(2,128)}), f32[2,8,256]{2,0,1:T(2,128)S(1)}, u32[]{:S(2)}, u32[]{:S(2)}) async-start(f32[2,8,256]{2,0,1:T(2,128)} %broadcast_select_fusion), calls=%async_computation.3 | async-start | bytes 32768 | tf_op jit(solution)/shard_map/all_to_all | solution.py:70
  361.3 61.5 %all-to-all-start.4 = ((f32[2,8,256]{2,0,1:T(2,128)}), f32[2,8,256]{2,0,1:T(2,128)S(1)}, u32[]{:S(2)}, u32[]{:S(2)}) async-start(f32[2,8,256]{2,0,1:T(2,128)} %pad_maximum_fusion), calls=%async_computation.4 | async-start | bytes 32768 | tf_op jit(solution)/shard_map/all_to_all | solution.py:135
  374.1 3.6 copy-start.6
  377.7 14.6 %copy-start.4 = (bf16[1024,256]{1,0:T(8,128)(2,1)S(1)}, bf16[1024,256]{1,0:T(8,128)(2,1)}, u32[]{:S(2)}) copy-start(bf16[1024,256]{1,0:T(8,128)(2,1)} %multiply_convert_fusion.1) | copy-start | bytes 1572868
  396.8 20.4 %copy-start.5 = (bf16[1024,256]{1,0:T(8,128)(2,1)S(1)}, bf16[1024,256]{1,0:T(8,128)(2,1)}, u32[]{:S(2)}) copy-start(bf16[1024,256]{1,0:T(8,128)(2,1)} %multiply_convert_fusion) | copy-start | bytes 1572868
  422.7 56.9 %copy-start.14 = (bf16[1024,1024]{1,0:T(8,128)(2,1)S(1)}, bf16[1024,1024]{1,0:T(8,128)(2,1)}, u32[]{:S(2)}) copy-start(bf16[1024,1024]{1,0:T(8,128)(2,1)} %all-gather.10.cloned.1.call-done) | copy-start | bytes 6291460
  422.7 144.3 %all-to-all-start.2 = ((f32[6,8,128,256]{3,2,0,1:T(8,128)}), f32[6,8,128,256]{3,2,0,1:T(8,128)}, u32[]{:S(2)}, u32[]{:S(2)}) async-start(f32[6,8,128,256]{3,2,0,1:T(8,128)} %constant_dynamic-update-slice_fusion), calls=%async_computation.2 | async-start | bytes 12582912 | tf_op jit(solution)/shard_map/all_to_all | solution.py:134
  428.4 26.3 %all-gather.22.cloned.1.call-start = ((), (), s32[]{:S(2)}) async-start(), calls=%async_computation.11 | async-start | bytes 2621440 | tf_op jit(solution)/shard_map/all_gather | solution.py:88
  429.1 50.5 %all-gather.20.cloned.1.call-start = ((), (), s32[]{:S(2)}) async-start(), calls=%async_computation.10 | async-start | bytes 2621440 | tf_op jit(solution)/shard_map/all_gather | solution.py:95
  578.5 3.6 copy-start.1
Sparse Core Ops, SparseCore 0:
  265.2 25.8 all-gather.23
  294.9 22.8 all-gather.11
  319.8 22.8 all-gather.15
  344.7 22.8 all-gather.9
  369.5 22.8 all-gather.13
  394.3 22.8 all-gather.17
  431.3 23.2 all-gather.21
  456.8 22.8 all-gather.19
where the time goes:
time: 590 us; the launch traced here: 589 us
  blocking collectives  262 us (44%)
  waiting for transfers between devices  199 us (34%)
  matrix products  50.6 us (9%)
  starting transfers between devices  22.5 us (4%)
  local copies, waits for them, and re-layouts  22.4 us (4%)
  between operations  19 us (3%)
  other arithmetic  13.2 us (2%)
    psum x1, blocking collectives, shards(): summed, norm_total = lax.psum((partial_value, norm_grads[0]), 'dp')  231 us
    all_to_all x1, waiting for transfers between devices, shards(): lax.all_to_all(back_stack, 'dp', split_axis=1, concat_axis=1, tiled=True)  82 us
    all_to_all x1, blocking collectives, shards(): lax.all_to_all(narrow_out, 'dp', split_axis=1, concat_axis=1, tiled=True)  31.4 us
    all_gather x1, waiting for transfers between devices, shards(): direction_full = lax.all_gather(direction, 'mp', axis=1, tiled=True)  25 us
    all_gather x1, waiting for transfers between devices, shards(): lax.all_gather(right_local, 'mp', axis=1, tiled=True)  22.2 us
    all_gather x1, waiting for transfers between devices, shards(): lax.all_gather(grad_b, 'mp', axis=1, tiled=True)  21.9 us
    all_gather x1, waiting for transfers between devices, shards(): lax.all_gather(iter_right, 'mp', axis=1, tiled=True)  19.3 us
    dot_general x3, matrix products, contract(): lax.dot_general(left, right, (((left_dim,), (right_dim,)), ((), ())), pre...  13.4 us
  transfers between devices with their start and end apart: 12, of which 9 were waited for; matrix products, arithmetic and copies ran while one was open for 10% of the time, Pallas kernels for 0%

commit v1 on v0

v1 whole, which is shorter than its diff:
```python
import jax
import jax.numpy as jnp
from jax import lax
from jax.sharding import PartitionSpec as P

FIX_ONE = 1.0 - 0.9**10
FIX_TWO = 1.0 - 0.95**10
BF = jnp.bfloat16
F32 = jnp.float32


def contract(left, right, left_dim, right_dim):
    return lax.dot_general(
        left, right, (((left_dim,), (right_dim,)), ((), ())), preferred_element_type=F32
    )


def to_tile(blocks):
    out = lax.all_to_all(blocks, "mp", split_axis=1, concat_axis=1, tiled=True)
    k, n, r, c = out.shape
    return out.transpose(0, 2, 1, 3).reshape(k, r, n * c)


def to_home(rows, n):
    k, r, c = rows.shape
    out = rows.reshape(k, r, n, c // n).transpose(0, 2, 1, 3)
    return lax.all_to_all(out, "mp", split_axis=1, concat_axis=1, tiled=True)


def gather_rows(rows):
    return lax.all_gather(rows, "dp", axis=0, tiled=True)


def normalize(power):
    wide = power.astype(F32)
    return lax.rsqrt(jnp.sum(wide * wide, axis=0, keepdims=True) + 1e-06)


def shards(
    features,
    out_grads,
    norm_grads,
    owners,
    moment1,
    moment2,
    left_stats,
    right_stats,
    left_basis,
    right_basis,
    norm_m,
    norm_v,
):
    dp = lax.axis_size("dp")
    tiles, slab, width = moment1.shape
    full = slab * dp
    me = lax.axis_index("dp")
    row0 = me * slab

    narrow = to_tile(jnp.stack([left_basis, right_basis, left_stats, right_stats]).astype(BF))
    left_full = gather_rows(narrow[0])
    right_full = gather_rows(narrow[1])

    flat = out_grads.reshape(out_grads.shape[0], tiles * width)
    partial = contract(features, flat, 0, 0).astype(BF).reshape(dp, slab, tiles * width)
    parts = lax.all_to_all(partial, "dp", split_axis=0, concat_axis=0, tiled=True)
    grad_home = jnp.sum(parts.astype(F32), axis=0).astype(BF)
    grad_home = grad_home.reshape(slab, tiles, width).transpose(1, 0, 2)
    grad_rows = to_tile(grad_home[None])[0]
    grad_full = gather_rows(grad_rows)

    wide = to_tile(jnp.stack([moment1, moment2]))

    prod_l = contract(grad_rows, grad_full, 1, 1)
    grad_cols = lax.dynamic_slice_in_dim(grad_full, row0, slab, 1)
    prod_r = contract(grad_cols, grad_full, 0, 0)
    stats_l = (0.95 * narrow[2].astype(F32) + 0.05 * prod_l).astype(BF)
    stats_r = (0.95 * narrow[3].astype(F32) + 0.05 * prod_r).astype(BF)
    power_l = contract(stats_l, left_full, 1, 0).astype(BF)
    power_r = contract(stats_r, right_full, 1, 0).astype(BF)
    power_l_full = gather_rows(power_l)
    power_r_full = gather_rows(power_r)

    left_cols = lax.dynamic_slice_in_dim(left_full, row0, slab, 1)
    half = contract(left_cols, grad_full, 0, 0).astype(BF)
    rotated = contract(half, right_full, 1, 0)
    tile_one = 0.9 * wide[0] + 0.1 * rotated
    tile_two = 0.95 * wide[1] + 0.05 * rotated * rotated
    direction = (tile_one / FIX_ONE / (jnp.sqrt(tile_two / FIX_TWO) + 1e-08)).astype(BF)
    back = contract(direction, right_full, 1, 1).astype(BF)
    back_full = gather_rows(back)

    home1 = to_home(jnp.stack([rotated, prod_l, prod_r]).astype(BF), tiles).astype(F32)
    new_one = 0.9 * moment1 + 0.1 * home1[0]
    new_two = 0.95 * moment2 + 0.05 * home1[0] * home1[0]
    new_sl = 0.95 * left_stats + 0.05 * home1[1]
    new_sr = 0.95 * right_stats + 0.05 * home1[2]

    update = contract(narrow[0], back_full, 1, 0).astype(BF)

    def refine(power_full, power_rows):
        scale = normalize(power_full)
        iter_full = (power_full.astype(F32) * scale).astype(BF)
        iter_rows = (power_rows.astype(F32) * scale).astype(BF)
        gram = contract(iter_rows, iter_full, 1, 1).astype(BF)
        return 1.5 * iter_rows.astype(F32) - 0.5 * contract(gram, iter_full, 1, 0)

    new_l = refine(power_l_full, power_l)
    new_r = refine(power_r_full, power_r)
    home2 = to_home(jnp.stack([new_l.astype(BF), new_r.astype(BF), update]), tiles)
    new_bl = home2[0].astype(F32)
    new_br = home2[1].astype(F32)
    slot_of = jnp.arange(dp, dtype=jnp.int32)[:, None, None]
    slots = jnp.zeros((dp, slab, width), BF)
    for n in range(tiles):
        slots = jnp.where(slot_of == owners[n], home2[2, n][None], slots)
    update_slot = lax.all_to_all(slots, "dp", split_axis=0, concat_axis=0, tiled=True)
    update_slot = update_slot.reshape(1, full, width)

    packed = jnp.concatenate([norm_grads[0], norm_m, norm_v])[None]
    everyone = lax.all_gather(packed, "dp", axis=0, tiled=True)
    size = norm_grads.shape[1]
    part = norm_m.shape[0]
    norm_total = jnp.sum(everyone[:, :size], axis=0)
    all_nm = 0.9 * everyone[:, size : size + part].reshape(size) + 0.1 * norm_total
    all_nv = (
        0.95 * everyone[:, size + part :].reshape(size) + 0.05 * norm_total * norm_total
    )
    norm_step = all_nm / FIX_ONE / (jnp.sqrt(all_nv / FIX_TWO) + 1e-08)
    norm_slot = jnp.where(me == owners[tiles], norm_step, 0.0)[None]
    new_nm = lax.dynamic_slice_in_dim(all_nm, me * part, part, 0)
    new_nv = lax.dynamic_slice_in_dim(all_nv, me * part, part, 0)
    return (
        new_one,
        new_two,
        new_sl,
        new_sr,
        new_bl,
        new_br,
        update_slot,
        new_nm,
        new_nv,
        norm_slot,
    )


def solution(mesh):
    in_specs = (
        P("dp", None),
        P("dp", None, "mp"),
        P("dp", None),
        P(),
        P(None, "dp", "mp"),
        P(None, "dp", "mp"),
        P(None, "dp", "mp"),
        P(None, "dp", "mp"),
        P(None, "dp", "mp"),
        P(None, "dp", "mp"),
        P("dp"),
        P("dp"),
    )
    out_specs = (
        P(None, "dp", "mp"),
        P(None, "dp", "mp"),
        P(None, "dp", "mp"),
        P(None, "dp", "mp"),
        P(None, "dp", "mp"),
        P(None, "dp", "mp"),
        P("dp", None, "mp"),
        P("dp"),
        P("dp"),
        P("dp", None),
    )
    return jax.shard_map(shards, mesh=mesh, in_specs=in_specs, out_specs=out_specs, check_vma=False)
```

time: 590 us -> 473 us (0.80)
  blocking collectives: 262 us -> 129 us
  waiting for transfers between devices: 199 us -> 241 us
  matrix products: 50.6 us -> 32 us
  starting transfers between devices: 22.5 us -> 11.6 us
  other arithmetic: 13.2 us -> 19.3 us
    psum x1 -> x0, blocking collectives: 231 us -> none  [shards(): summed, norm_total = lax.psum((partial_value, norm_grads[0]), 'dp')]
    all_gather x8 -> x6, waiting for transfers between devices: 110 us -> 222 us  [gather_rows(): return lax.all_gather(rows, 'dp', axis=0, tiled=True)]
    all_to_all x4 -> x3, waiting for transfers between devices: 88 us -> 17.8 us  [the longest x1 9.82 us: shards(): lax.all_to_all(slots, 'dp', split_axis=0, concat_axis=0, tiled=True)]
    all_to_all x1 -> x4, blocking collectives: 31.4 us -> 98.3 us  [the longest x1 55.4 us: shards(): lax.all_to_all(partial, 'dp', split_axis=0, concat_axis=0, tiled=True)]
    dot_general x9 -> x0, matrix products: 37.2 us -> none  [the longest x1 9.11 us: shards(): jnp.einsum('dn,kdrc->knrc', chooser, returned, precision=lax.Precision.HI...]
    all_gather x0 -> x1, blocking collectives: none -> 30.5 us  [shards(): everyone = lax.all_gather(packed, 'dp', axis=0, tiled=True)]
    dot_general x3 -> x10, matrix products: 13.4 us -> 32 us  [contract(): lax.dot_general(left, right, (((left_dim,), (right_dim,)), ((), ())), pre...]
    all_to_all x4 -> x3, starting transfers between devices: 21.8 us -> 11.3 us  [the longest x2 7.81 us: to_home(): return lax.all_to_all(out, 'mp', split_axis=1, concat_axis=1, tiled=True)]
  transfers between devices with their start and end apart: 12 -> 9, of which waited for: 9 -> 8; matrix products, arithmetic and copies ran while one was open for 10% -> 13% of each run, Pallas kernels for 0% -> 0%
where the time goes in v1:
time: 473 us; the launch traced here: 471 us
  waiting for transfers between devices  241 us (51%)
  blocking collectives  129 us (27%)
  matrix products  32 us (7%)
  local copies, waits for them, and re-layouts  23.3 us (5%)
  other arithmetic  19.3 us (4%)
  between operations  15.3 us (3%)
  starting transfers between devices  11.6 us (2%)
    all_gather x6, waiting for transfers between devices, gather_rows(): return lax.all_gather(rows, 'dp', axis=0, tiled=True)  222 us
    all_to_all x1, blocking collectives, shards(): lax.all_to_all(partial, 'dp', split_axis=0, concat_axis=0, tiled=True)  55.4 us
    all_to_all x3, blocking collectives, to_tile(): out = lax.all_to_all(blocks, 'mp', split_axis=1, concat_axis=1, tiled=True)  42.9 us
    dot_general x10, matrix products, contract(): lax.dot_general(left, right, (((left_dim,), (right_dim,)), ((), ())), pre...  32 us
    all_gather x1, blocking collectives, shards(): everyone = lax.all_gather(packed, 'dp', axis=0, tiled=True)  30.5 us
    all_to_all x1, waiting for transfers between devices, shards(): lax.all_to_all(slots, 'dp', split_axis=0, concat_axis=0, tiled=True)  9.82 us
  transfers between devices with their start and end apart: 9, of which 8 were waited for; matrix products, arithmetic and copies ran while one was open for 13% of the time, Pallas kernels for 0%

profile of v1, /device:TPU:0, one launch (start us, length us, event | category | flops | bytes accessed | tf_op | source)
XLA Modules:
  0.0 471.3 jit_solution(4801705262632254614)
XLA Ops:
  7.2 2.2 copy.123
  9.5 2.4 convolution_convert_fusion
  11.9 55.4 %all_to_all.35 = bf16[8,128,1024]{2,1,0:T(8,128)(2,1)} all-to-all(bf16[8,128,1024]{2,1,0:T(8,128)(2,1)S(1)} %bitcast.132), channel_id=1, replica_groups=mesh['dp'=8,'mp'=4] {'dp'}, dimensions={0} | all-to-all | bytes 4194304 | tf_op jit(solution)/shard_map/all_to_all | solution.py:65
  67.3 2.0 reduce_sum.41
  69.4 0.8 copy.97
  70.2 1.1 copy.98
  71.3 9.1 %all_to_all.36 = bf16[1,4,128,256]{3,2,0,1:T(8,128)(2,1)} all-to-all(bf16[1,4,128,256]{3,2,0,1:T(8,128)(2,1)S(1)} %copy.98), channel_id=1, replica_groups=mesh['dp'=8,'mp'=4] {'mp'}, dimensions={1} | all-to-all | bytes 524288 | tf_op jit(solution)/shard_map/all_to_all | solution.py:19
  80.3 1.8 copy.99
  82.6 1.2 copy.93
  83.8 1.2 copy.92
  85.2 16.9 %all_to_all.37 = bf16[4,4,128,256]{2,3,0,1:T(8,128)(2,1)S(1)} all-to-all(bf16[4,4,128,256]{2,3,0,1:T(8,128)(2,1)S(1)} %pad_maximum_fusion), channel_id=1, replica_groups=mesh['dp'=8,'mp'=4] {'mp'}, dimensions={1} | all-to-all | bytes 2097152 | tf_op jit(solution)/shard_map/all_to_all | solution.py:19
  102.1 0.8 fusion.87
  103.0 0.7 all-gather.9.cloned.1.call-update
  103.8 1.1 convert_multiply_fusion.5
  104.8 1.2 copy.117
  106.1 24.6 %all-gather.11.cloned.1.call-done = bf16[1024,1024]{0,1:T(8,128)(2,1)} async-done(((bf16[128,1024]{0,1:T(8,128)(2,1)}), bf16[1024,1024]{0,1:T(8,128)(2,1)}) %all-gather.11.cloned.1.call-update) | async-done | bytes 2097168 | tf_op jit(solution)/shard_map/all_gather | solution.py:31
  130.6 3.4 fusion.89
  134.0 47.8 %all-gather.13.cloned.1.call-done = bf16[1024,1024]{0,1:T(8,128)(2,1)} async-done(((bf16[128,1024]{0,1:T(8,128)(2,1)}), bf16[1024,1024]{0,1:T(8,128)(2,1)}) %all-gather.13.cloned.1.call-update) | async-done | bytes 2097168 | tf_op jit(solution)/shard_map/all_gather | solution.py:31
  181.8 3.3 convolution_convert_fusion.3
  185.2 0.2 copy.116
  185.5 2.8 fusion.90
  188.2 44.8 %all-gather.9.cloned.1.call-done = bf16[1024,1024]{0,1:T(8,128)(2,1)} async-done(((bf16[128,1024]{0,1:T(8,128)(2,1)}), bf16[1024,1024]{0,1:T(8,128)(2,1)}) %all-gather.9.cloned.1.call-update) | async-done | bytes 2097168 | tf_op jit(solution)/shard_map/all_gather | solution.py:31
  233.0 3.1 convolution_convert_fusion.4
  236.2 1.2 copy.108
  237.5 1.2 copy.109
  238.8 17.0 %all_to_all.38 = f32[2,4,128,256]{2,3,0,1:T(8,128)S(1)} all-to-all(f32[2,4,128,256]{2,3,0,1:T(8,128)S(1)} %pad_maximum_fusion.1), channel_id=1, replica_groups=mesh['dp'=8,'mp'=4] {'mp'}, dimensions={1} | all-to-all | bytes 2097152 | tf_op jit(solution)/shard_map/all_to_all | solution.py:19
  255.9 1.0 copy.118
  256.9 0.2 copy.119
  257.2 4.8 %fusion.91 = (bf16[128,1024]{1,0:T(8,128)(2,1)}, f32[128,1024]{1,0:T(8,128)}) fusion(bf16[1024,1024]{0,1:T(8,128)(2,1)} %all-gather.13.cloned.1.call-done, bf16[1024,1024]{0,1:T(8,128)(2,1)} %all-gather.11.cloned.1.call-done, bf16[1024,1024]{0,1:T(8,128)(2,1)} %all-gather.9.cloned.1.call-done, s32[]{:T(128)S(6)} %select_n.36), kind=kOutput, calls=%fused_computation.119 | convolution fusion | flops 537133056 | bytes 5242884 | tf_op jit(solution)/shard_map/dot_general | solution.py:13
  261.9 3.1 convolution_convert_fusion.2
  265.2 0.6 fusion.88
  265.8 17.1 %all-gather.17.cloned.1.call-done = bf16[1024,1024]{1,0:T(8,128)(2,1)} async-done(((bf16[128,1024]{1,0:T(8,128)(2,1)}), bf16[1024,1024]{1,0:T(8,128)(2,1)}) %all-gather.17.cloned.1.call-update) | async-done | bytes 2097168 | tf_op jit(solution)/shard_map/all_gather | solution.py:31
  282.9 2.1 fusion.2
  285.0 3.5 fusion.24
  288.5 0.2 stack.63
  288.7 43.9 %all-gather.15.cloned.1.call-done = bf16[1024,1024]{1,0:T(8,128)(2,1)} async-done(((bf16[128,1024]{1,0:T(8,128)(2,1)}), bf16[1024,1024]{1,0:T(8,128)(2,1)}) %all-gather.15.cloned.1.call-update) | async-done | bytes 2097168 | tf_op jit(solution)/shard_map/all_gather | solution.py:31
  332.5 2.1 fusion
  334.6 3.5 fusion.27
  338.1 0.2 stack.62
  338.4 44.4 %all-gather.19.cloned.1.call-done = bf16[1024,1024]{1,0:T(8,128)(2,1)} async-done(((bf16[128,1024]{1,0:T(8,128)(2,1)}), bf16[1024,1024]{1,0:T(8,128)(2,1)}) %all-gather.19.cloned.1.call-update) | async-done | bytes 2097168 | tf_op jit(solution)/shard_map/all_gather | solution.py:31
  382.7 2.1 convolution_convert_fusion.1
  384.8 0.2 stack.67
  385.0 1.0 maximum_bitcast_fusion.1
  386.0 3.6 all-to-all-start.5
  389.7 30.5 %all-gather.1 = f32[8,1,2560]{2,1,0:T(1,128)S(1)} all-gather(f32[1,1,2560]{2,1,0:T(1,128)S(1)} %reshape.191), channel_id=2, replica_groups=mesh['dp'=8,'mp'=4] {'dp'}, dimensions={0}, use_global_device_ids=true | all-gather | bytes 92160 | tf_op jit(solution)/shard_map/all_gather | solution.py:120
  420.2 1.3 iota_compare_fusion
  421.6 1.8 stack.58
  423.4 1.7 copy.100
  425.1 0.9 stack.60
  426.0 1.7 copy.102
  427.6 0.2 stack.59
  427.9 2.0 maximum_bitcast_fusion
  429.9 4.2 all-to-all-start.3
  434.1 1.3 iota_compare_fusion.2
  436.1 0.7 fusion.76
  436.7 1.1 select_select_fusion
  437.8 8.0 %all-to-all-done.3 = bf16[3,4,128,256]{3,2,0,1:T(8,128)(2,1)} async-done(((bf16[3,4,128,256]{3,2,0,1:T(8,128)(2,1)}), bf16[3,4,128,256]{3,2,0,1:T(8,128)(2,1)}, u32[]{:S(2)}, u32[]{:S(2)}) %all-to-all-start.3) | async-done | bytes 786464 | tf_op jit(solution)/shard_map/all_to_all | solution.py:27
  445.8 3.5 all-to-all-start.6
  449.3 0.7 broadcast_select_fusion
  450.0 1.3 convert_element_type.101
  451.3 1.5 fusion.48
  452.8 1.1 fusion.54
  453.8 9.8 %all-to-all-done.6 = bf16[8,128,256]{2,1,0:T(8,128)(2,1)S(1)} async-done(((bf16[8,128,256]{2,1,0:T(8,128)(2,1)}), bf16[8,128,256]{2,1,0:T(8,128)(2,1)S(1)}, u32[]{:S(2)}, u32[]{:S(2)}) %all-to-all-start.6) | async-done | bytes 524320 | tf_op jit(solution)/shard_map/all_to_all | solution.py:116
  463.7 0.8 copy.135
  (73 shorter events, 1.5 us)
Async XLA Ops:
  7.2 2.3 copy-start
  7.2 123.5 %all-gather.11.cloned.1.call-start = ((), (), s32[]{:S(2)}) async-start(), calls=%async_computation.8 | async-start | bytes 2359296 | tf_op jit(solution)/shard_map/all_gather | solution.py:31
  67.3 14.9 %copy-start.4 = (f32[4,128,256]{2,1,0:T(8,128)S(1)}, f32[4,128,256]{2,1,0:T(8,128)}, u32[]{:S(2)}) copy-start(f32[4,128,256]{2,1,0:T(8,128)} %param.19) | copy-start | bytes 1572868
  69.3 13.1 %copy-start.6 = (f32[4,128,256]{2,1,0:T(8,128)S(1)}, f32[4,128,256]{2,1,0:T(8,128)}, u32[]{:S(2)}) copy-start(f32[4,128,256]{2,1,0:T(8,128)} %param.18) | copy-start | bytes 1572868
  82.2 99.7 %all-gather.13.cloned.1.call-start = ((), (), s32[]{:S(2)}) async-start(), calls=%async_computation.9 | async-start | bytes 2359296 | tf_op jit(solution)/shard_map/all_gather | solution.py:31
  103.0 130.1 %all-gather.9.cloned.1.call-start = ((), (), s32[]{:S(2)}) async-start(), calls=%async_computation.7 | async-start | bytes 2359296 | tf_op jit(solution)/shard_map/all_gather | solution.py:31
  103.7 179.2 %all-gather.17.cloned.1.call-start = ((), (), s32[]{:S(2)}) async-start(), calls=%async_computation.11 | async-start | bytes 2359296 | tf_op jit(solution)/shard_map/all_gather | solution.py:31
  134.0 51.2 %copy-start.3 = (f32[1,128,4,256]{1,3,2,0:T(8,128)S(1)}, f32[1,128,4,256]{1,3,2,0:T(8,128)}, u32[]{:S(2)}) copy-start(f32[1,128,4,256]{1,3,2,0:T(8,128)} %get-tuple-element.14) | copy-start | bytes 1572868
  181.8 3.6 copy-start.1
  185.2 147.4 %all-gather.15.cloned.1.call-start = ((), (), s32[]{:S(2)}) async-start(), calls=%async_computation.10 | async-start | bytes 2359296 | tf_op jit(solution)/shard_map/all_gather | solution.py:31
  236.2 146.6 %all-gather.19.cloned.1.call-start = ((), (), s32[]{:S(2)}) async-start(), calls=%async_computation.12 | async-start | bytes 2359296 | tf_op jit(solution)/shard_map/all_gather | solution.py:31
  257.1 4.8 %copy-start.14 = (f32[128,1024]{1,0:T(8,128)S(1)}, f32[128,1024]{1,0:T(8,128)}, u32[]{:S(2)}) copy-start(f32[128,1024]{1,0:T(8,128)} %copy.118) | copy-start | bytes 1572868
  261.9 3.2 copy-start.16
  261.9 3.2 copy-start.17
  261.9 3.2 copy-start.18
  261.9 3.2 copy-start.15
  265.1 19.9 %copy-start.12 = (bf16[128,1024]{1,0:T(8,128)(2,1)S(1)}, bf16[128,1024]{1,0:T(8,128)(2,1)}, u32[]{:S(2)}) copy-start(bf16[128,1024]{1,0:T(8,128)(2,1)} %convolution_convert_fusion.3) | copy-start | bytes 786436
  288.4 46.2 %copy-start.13 = (bf16[128,1024]{1,0:T(8,128)(2,1)S(1)}, bf16[128,1024]{1,0:T(8,128)(2,1)}, u32[]{:S(2)}) copy-start(bf16[128,1024]{1,0:T(8,128)(2,1)} %convolution_convert_fusion.4) | copy-start | bytes 786436
  334.6 48.1 %copy-start.2 = (bf16[1,128,4,256]{1,3,2,0:T(8,128)(2,1)S(1)}, bf16[1,128,4,256]{1,3,2,0:T(8,128)(2,1)}, u32[]{:S(2)}) copy-start(bf16[1,128,4,256]{1,3,2,0:T(8,128)(2,1)} %get-tuple-element.18) | copy-start | bytes 786436
  385.0 40.0 %copy-start.10 = (bf16[128,1024]{1,0:T(8,128)(2,1)S(1)}, bf16[128,1024]{1,0:T(8,128)(2,1)}, u32[]{:S(2)}) copy-start(bf16[128,1024]{1,0:T(8,128)(2,1)} %get-tuple-element.37) | copy-start | bytes 786436
  386.0 41.6 %copy-start.11 = (bf16[128,1024]{1,0:T(8,128)(2,1)S(1)}, bf16[128,1024]{1,0:T(8,128)(2,1)}, u32[]{:S(2)}) copy-start(bf16[128,1024]{1,0:T(8,128)(2,1)} %get-tuple-element.39) | copy-start | bytes 786436
  386.0 43.9 %all-to-all-start.5 = ((bf16[3,4,128,256]{3,2,0,1:T(8,128)(2,1)}), bf16[3,4,128,256]{3,2,0,1:T(8,128)(2,1)S(1)}, u32[]{:S(2)}, u32[]{:S(2)}) async-start(bf16[3,4,128,256]{3,2,0,1:T(8,128)(2,1)} %maximum_bitcast_fusion.1), calls=%async_computation.5 | async-start | bytes 1572864 | tf_op jit(solution)/shard_map/all_to_all | solution.py:27
  429.9 15.9 %all-to-all-start.3 = ((bf16[3,4,128,256]{3,2,0,1:T(8,128)(2,1)}), bf16[3,4,128,256]{3,2,0,1:T(8,128)(2,1)}, u32[]{:S(2)}, u32[]{:S(2)}) async-start(bf16[3,4,128,256]{3,2,0,1:T(8,128)(2,1)} %maximum_bitcast_fusion), calls=%async_computation.3 | async-start | bytes 1572864 | tf_op jit(solution)/shard_map/all_to_all | solution.py:27
  445.8 17.9 %all-to-all-start.6 = ((bf16[8,128,256]{2,1,0:T(8,128)(2,1)}), bf16[8,128,256]{2,1,0:T(8,128)(2,1)S(1)}, u32[]{:S(2)}, u32[]{:S(2)}) async-start(bf16[8,128,256]{2,1,0:T(8,128)(2,1)} %select_select_fusion), calls=%async_computation.6 | async-start | bytes 1048576 | tf_op jit(solution)/shard_map/all_to_all | solution.py:116
  449.3 2.0 copy-start.5
  449.3 2.0 copy-start.7
  449.3 2.0 copy-start.8
  449.3 2.0 copy-start.9
Sparse Core Ops, SparseCore 0:
  82.3 48.3 all-gather.10
  133.3 48.5 all-gather.12
  184.5 48.5 all-gather.8
  235.6 47.2 all-gather.16
  284.9 47.6 all-gather.14
  335.1 47.6 all-gather.18

commit v2 on v1

--- a/solution.py
+++ b/solution.py
@@ -116,19 +116,16 @@
     update_slot = lax.all_to_all(slots, "dp", split_axis=0, concat_axis=0, tiled=True)
     update_slot = update_slot.reshape(1, full, width)
 
-    packed = jnp.concatenate([norm_grads[0], norm_m, norm_v])[None]
-    everyone = lax.all_gather(packed, "dp", axis=0, tiled=True)
-    size = norm_grads.shape[1]
-    part = norm_m.shape[0]
-    norm_total = jnp.sum(everyone[:, :size], axis=0)
-    all_nm = 0.9 * everyone[:, size : size + part].reshape(size) + 0.1 * norm_total
-    all_nv = (
-        0.95 * everyone[:, size + part :].reshape(size) + 0.05 * norm_total * norm_total
-    )
-    norm_step = all_nm / FIX_ONE / (jnp.sqrt(all_nv / FIX_TWO) + 1e-08)
-    norm_slot = jnp.where(me == owners[tiles], norm_step, 0.0)[None]
-    new_nm = lax.dynamic_slice_in_dim(all_nm, me * part, part, 0)
-    new_nv = lax.dynamic_slice_in_dim(all_nv, me * part, part, 0)
+    norm_parts = norm_grads.reshape(dp, norm_m.shape[0])
+    norm_parts = lax.all_to_all(norm_parts, "dp", split_axis=0, concat_axis=0, tiled=True)
+    norm_total = jnp.sum(norm_parts, axis=0)
+    new_nm = 0.9 * norm_m + 0.1 * norm_total
+    new_nv = 0.95 * norm_v + 0.05 * norm_total * norm_total
+    norm_step = new_nm / FIX_ONE / (jnp.sqrt(new_nv / FIX_TWO) + 1e-08)
+    to_owner = (jnp.arange(dp, dtype=jnp.int32) == owners[tiles])[:, None]
+    norm_out = jnp.where(to_owner, norm_step[None], 0.0)
+    norm_slot = lax.all_to_all(norm_out, "dp", split_axis=0, concat_axis=0, tiled=True)
+    norm_slot = norm_slot.reshape(1, -1)
     return (
         new_one,
         new_two,

time: 473 us -> 445 us (0.941)
  blocking collectives: 129 us -> 98.3 us
  starting transfers between devices: 11.6 us -> 18.5 us
  waiting for transfers between devices: 241 us -> 236 us
    all_gather x1 -> x0, blocking collectives: 30.5 us -> none  [shards(): everyone = lax.all_gather(packed, 'dp', axis=0, tiled=True)]
    all_gather x6, waiting for transfers between devices: 222 us -> 208 us  [gather_rows(): return lax.all_gather(rows, 'dp', axis=0, tiled=True)]
    all_to_all x0 -> x2, starting transfers between devices: none -> 6.99 us  [the longest x1 3.51 us: shards(): lax.all_to_all(norm_out, 'dp', split_axis=0, concat_axis=0, tiled=True)]
    all_to_all x0 -> x2, waiting for transfers between devices: none -> 5.23 us  [the longest x1 5.23 us: shards(): lax.all_to_all(norm_parts, 'dp', split_axis=0, concat_axis=0, tiled=True)]
  transfers between devices with their start and end apart: 9 -> 11, of which waited for: 8 -> 10; matrix products, arithmetic and copies ran while one was open for 13% -> 14% of each run, Pallas kernels for 0% -> 0%
where the time goes in v2:
time: 445 us; the launch traced here: 443 us
  waiting for transfers between devices  236 us (53%)
  blocking collectives  98.3 us (22%)
  matrix products  32 us (7%)
  local copies, waits for them, and re-layouts  24.2 us (5%)
  other arithmetic  20 us (4%)
  starting transfers between devices  18.5 us (4%)
  between operations  14.6 us (3%)
    all_gather x6, waiting for transfers between devices, gather_rows(): return lax.all_gather(rows, 'dp', axis=0, tiled=True)  208 us
    all_to_all x1, blocking collectives, shards(): lax.all_to_all(partial, 'dp', split_axis=0, concat_axis=0, tiled=True)  55.4 us
    all_to_all x3, blocking collectives, to_tile(): out = lax.all_to_all(blocks, 'mp', split_axis=1, concat_axis=1, tiled=True)  42.9 us
    dot_general x10, matrix products, contract(): lax.dot_general(left, right, (((left_dim,), (right_dim,)), ((), ())), pre...  32 us
    all_to_all x2, waiting for transfers between devices, to_home(): return lax.all_to_all(out, 'mp', split_axis=1, concat_axis=1, tiled=True)  11.3 us
    all_to_all x1, waiting for transfers between devices, shards(): lax.all_to_all(slots, 'dp', split_axis=0, concat_axis=0, tiled=True)  10.1 us
    unnamed x45, local copies, waits for them, and re-layouts  9.22 us
  transfers between devices with their start and end apart: 11, of which 10 were waited for; matrix products, arithmetic and copies ran while one was open for 14% of the time, Pallas kernels for 0%

profile of v2, /device:TPU:0, one launch (start us, length us, event | category | flops | bytes accessed | tf_op | source)
XLA Modules:
  0.0 443.4 jit_solution(10692234722072050169)
XLA Ops:
  7.2 2.2 copy.122
  9.5 2.4 convolution_convert_fusion
  11.9 55.4 %all_to_all.50 = bf16[8,128,1024]{2,1,0:T(8,128)(2,1)} all-to-all(bf16[8,128,1024]{2,1,0:T(8,128)(2,1)S(1)} %bitcast.115), channel_id=1, replica_groups=mesh['dp'=8,'mp'=4] {'dp'}, dimensions={0} | all-to-all | bytes 4194304 | tf_op jit(solution)/shard_map/all_to_all | solution.py:65
  67.3 2.0 reduce_sum.39
  69.4 0.8 copy.97
  70.2 1.1 copy.98
  71.3 9.1 %all_to_all.51 = bf16[1,4,128,256]{3,2,0,1:T(8,128)(2,1)} all-to-all(bf16[1,4,128,256]{3,2,0,1:T(8,128)(2,1)S(1)} %copy.98), channel_id=1, replica_groups=mesh['dp'=8,'mp'=4] {'mp'}, dimensions={1} | all-to-all | bytes 524288 | tf_op jit(solution)/shard_map/all_to_all | solution.py:19
  80.4 1.8 copy.99
  82.6 1.2 copy.93
  83.8 1.2 copy.92
  85.2 16.9 %all_to_all.52 = bf16[4,4,128,256]{2,3,0,1:T(8,128)(2,1)S(1)} all-to-all(bf16[4,4,128,256]{2,3,0,1:T(8,128)(2,1)S(1)} %pad_maximum_fusion), channel_id=1, replica_groups=mesh['dp'=8,'mp'=4] {'mp'}, dimensions={1} | all-to-all | bytes 2097152 | tf_op jit(solution)/shard_map/all_to_all | solution.py:19
  102.1 0.8 fusion.83
  103.0 0.7 all-gather.7.cloned.1.call-update
  103.8 1.1 convert_multiply_fusion.5
  104.8 1.2 copy.117
  106.1 24.6 %all-gather.9.cloned.1.call-done = bf16[1024,1024]{0,1:T(8,128)(2,1)} async-done(((bf16[128,1024]{0,1:T(8,128)(2,1)}), bf16[1024,1024]{0,1:T(8,128)(2,1)}) %all-gather.9.cloned.1.call-update) | async-done | bytes 2097168 | tf_op jit(solution)/shard_map/all_gather | solution.py:31
  130.7 3.4 fusion.85
  134.1 47.8 %all-gather.11.cloned.1.call-done = bf16[1024,1024]{0,1:T(8,128)(2,1)} async-done(((bf16[128,1024]{0,1:T(8,128)(2,1)}), bf16[1024,1024]{0,1:T(8,128)(2,1)}) %all-gather.11.cloned.1.call-update) | async-done | bytes 2097168 | tf_op jit(solution)/shard_map/all_gather | solution.py:31
  181.8 3.3 convolution_convert_fusion.3
  185.3 0.2 copy.116
  185.5 2.8 fusion.86
  188.2 44.8 %all-gather.7.cloned.1.call-done = bf16[1024,1024]{0,1:T(8,128)(2,1)} async-done(((bf16[128,1024]{0,1:T(8,128)(2,1)}), bf16[1024,1024]{0,1:T(8,128)(2,1)}) %all-gather.7.cloned.1.call-update) | async-done | bytes 2097168 | tf_op jit(solution)/shard_map/all_gather | solution.py:31
  233.0 3.1 convolution_convert_fusion.4
  236.2 1.2 copy.108
  237.4 1.2 copy.109
  238.8 17.0 %all_to_all.53 = f32[2,4,128,256]{2,3,0,1:T(8,128)S(1)} all-to-all(f32[2,4,128,256]{2,3,0,1:T(8,128)S(1)} %pad_maximum_fusion.1), channel_id=1, replica_groups=mesh['dp'=8,'mp'=4] {'mp'}, dimensions={1} | all-to-all | bytes 2097152 | tf_op jit(solution)/shard_map/all_to_all | solution.py:19
  255.9 1.0 copy.118
  257.1 4.8 %fusion.87 = (bf16[128,1024]{1,0:T(8,128)(2,1)}, f32[128,1024]{1,0:T(8,128)}) fusion(bf16[1024,1024]{0,1:T(8,128)(2,1)} %all-gather.11.cloned.1.call-done, bf16[1024,1024]{0,1:T(8,128)(2,1)} %all-gather.9.cloned.1.call-done, bf16[1024,1024]{0,1:T(8,128)(2,1)} %all-gather.7.cloned.1.call-done, s32[]{:T(128)S(6)} %select_n.28), kind=kOutput, calls=%fused_computation.109 | convolution fusion | flops 537133056 | bytes 5242884 | tf_op jit(solution)/shard_map/dot_general | solution.py:13
  261.9 3.1 convolution_convert_fusion.2
  265.1 3.5 all-to-all-start.7
  268.6 0.7 fusion.84
  269.3 0.7 iota_compare_fusion
  269.9 5.2 %all-to-all-done.7 = f32[8,1,256]{2,1,0:T(1,128)S(1)} async-done(((f32[8,1,256]{2,1,0:T(1,128)}), f32[8,1,256]{2,1,0:T(1,128)S(1)}, u32[]{:S(2)}, u32[]{:S(2)}) %all-to-all-start.7) | async-done | bytes 8224 | tf_op jit(solution)/shard_map/all_to_all | solution.py:120
  275.2 0.6 add_divide_fusion
  275.8 0.7 broadcast_select_fusion
  276.4 3.5 all-to-all-start.8
  280.0 3.1 all-gather.15.cloned.1.call-done
  283.1 2.1 fusion.2
  285.1 3.5 fusion.24
  288.9 43.8 %all-gather.13.cloned.1.call-done = bf16[1024,1024]{1,0:T(8,128)(2,1)} async-done(((bf16[128,1024]{1,0:T(8,128)(2,1)}), bf16[1024,1024]{1,0:T(8,128)(2,1)}) %all-gather.13.cloned.1.call-update) | async-done | bytes 2097168 | tf_op jit(solution)/shard_map/all_gather | solution.py:31
  332.7 2.1 fusion
  334.8 3.5 fusion.27
  338.5 44.4 %all-gather.17.cloned.1.call-done = bf16[1024,1024]{1,0:T(8,128)(2,1)} async-done(((bf16[128,1024]{1,0:T(8,128)(2,1)}), bf16[1024,1024]{1,0:T(8,128)(2,1)}) %all-gather.17.cloned.1.call-update) | async-done | bytes 2097168 | tf_op jit(solution)/shard_map/all_gather | solution.py:31
  382.9 2.1 convolution_convert_fusion.1
  385.2 1.0 maximum_bitcast_fusion.1
  386.2 3.6 all-to-all-start.5
  389.8 1.8 stack.58
  391.6 1.7 copy.100
  393.3 0.9 stack.60
  394.2 1.7 copy.102
  396.1 2.0 maximum_bitcast_fusion
  398.1 3.3 all-to-all-done.5
  401.4 4.2 all-to-all-start.3
  405.6 1.3 iota_compare_fusion.1
  406.9 1.2 iota_compare_fusion.3
  408.1 1.1 select_select_fusion
  409.2 8.1 %all-to-all-done.3 = bf16[3,4,128,256]{3,2,0,1:T(8,128)(2,1)} async-done(((bf16[3,4,128,256]{3,2,0,1:T(8,128)(2,1)}), bf16[3,4,128,256]{3,2,0,1:T(8,128)(2,1)}, u32[]{:S(2)}, u32[]{:S(2)}) %all-to-all-start.3) | async-done | bytes 786464 | tf_op jit(solution)/shard_map/all_to_all | solution.py:27
  417.3 3.5 all-to-all-start.6
  420.8 1.4 convert_element_type.101
  422.5 1.5 fusion.48
  424.0 1.1 fusion.54
  425.1 10.1 %all-to-all-done.6 = bf16[8,128,256]{2,1,0:T(8,128)(2,1)S(1)} async-done(((bf16[8,128,256]{2,1,0:T(8,128)(2,1)}), bf16[8,128,256]{2,1,0:T(8,128)(2,1)S(1)}, u32[]{:S(2)}, u32[]{:S(2)}) %all-to-all-start.6) | async-done | bytes 524320 | tf_op jit(solution)/shard_map/all_to_all | solution.py:116
  435.1 0.8 copy.129
  435.9 0.6 copy.130
  (68 shorter events, 2.6 us)
Async XLA Ops:
  7.2 2.3 copy-start
  7.2 123.5 %all-gather.9.cloned.1.call-start = ((), (), s32[]{:S(2)}) async-start(), calls=%async_computation.10 | async-start | bytes 2359296 | tf_op jit(solution)/shard_map/all_gather | solution.py:31
  67.3 14.9 %copy-start.4 = (f32[4,128,256]{2,1,0:T(8,128)S(1)}, f32[4,128,256]{2,1,0:T(8,128)}, u32[]{:S(2)}) copy-start(f32[4,128,256]{2,1,0:T(8,128)} %param.19) | copy-start | bytes 1572868
  69.3 13.1 %copy-start.6 = (f32[4,128,256]{2,1,0:T(8,128)S(1)}, f32[4,128,256]{2,1,0:T(8,128)}, u32[]{:S(2)}) copy-start(f32[4,128,256]{2,1,0:T(8,128)} %param.18) | copy-start | bytes 1572868
  82.2 99.7 %all-gather.11.cloned.1.call-start = ((), (), s32[]{:S(2)}) async-start(), calls=%async_computation.11 | async-start | bytes 2359296 | tf_op jit(solution)/shard_map/all_gather | solution.py:31
  103.0 130.1 %all-gather.7.cloned.1.call-start = ((), (), s32[]{:S(2)}) async-start(), calls=%async_computation.9 | async-start | bytes 2359296 | tf_op jit(solution)/shard_map/all_gather | solution.py:31
  103.7 179.4 %all-gather.15.cloned.1.call-start = ((), (), s32[]{:S(2)}) async-start(), calls=%async_computation.13 | async-start | bytes 2359296 | tf_op jit(solution)/shard_map/all_gather | solution.py:31
  134.0 51.2 %copy-start.3 = (f32[1,128,4,256]{1,3,2,0:T(8,128)S(1)}, f32[1,128,4,256]{1,3,2,0:T(8,128)}, u32[]{:S(2)}) copy-start(f32[1,128,4,256]{1,3,2,0:T(8,128)} %get-tuple-element.17) | copy-start | bytes 1572868
  181.8 3.6 copy-start.1
  185.2 147.5 %all-gather.13.cloned.1.call-start = ((), (), s32[]{:S(2)}) async-start(), calls=%async_computation.12 | async-start | bytes 2359296 | tf_op jit(solution)/shard_map/all_gather | solution.py:31
  236.2 146.7 %all-gather.17.cloned.1.call-start = ((), (), s32[]{:S(2)}) async-start(), calls=%async_computation.14 | async-start | bytes 2359296 | tf_op jit(solution)/shard_map/all_gather | solution.py:31
  257.1 4.8 %copy-start.14 = (f32[128,1024]{1,0:T(8,128)S(1)}, f32[128,1024]{1,0:T(8,128)}, u32[]{:S(2)}) copy-start(f32[128,1024]{1,0:T(8,128)} %copy.118) | copy-start | bytes 1572868
  261.9 6.7 %copy-start.15 = (s32[5]{0:T(128)S(1)}, s32[5]{0:T(128)}, u32[]{:S(2)}) copy-start(s32[5]{0:T(128)} %param.15) | copy-start | bytes 64
  261.9 13.3 %copy-start.16 = (f32[256]{0:T(256)S(1)}, f32[256]{0:T(256)}, u32[]{:S(2)}) copy-start(f32[256]{0:T(256)} %param.23) | copy-start | bytes 3076
  261.9 13.3 %copy-start.17 = (f32[256]{0:T(256)S(1)}, f32[256]{0:T(256)}, u32[]{:S(2)}) copy-start(f32[256]{0:T(256)} %param.22) | copy-start | bytes 3076
  265.1 20.1 %copy-start.12 = (bf16[128,1024]{1,0:T(8,128)(2,1)S(1)}, bf16[128,1024]{1,0:T(8,128)(2,1)}, u32[]{:S(2)}) copy-start(bf16[128,1024]{1,0:T(8,128)(2,1)} %convolution_convert_fusion.3) | copy-start | bytes 786436
  265.1 10.1 %all-to-all-start.7 = ((f32[8,1,256]{2,1,0:T(1,128)}), f32[8,1,256]{2,1,0:T(1,128)S(1)}, u32[]{:S(2)}, u32[]{:S(2)}) async-start(f32[8,1,256]{2,1,0:T(1,128)} %bitcast.38), calls=%async_computation.7 | async-start | bytes 16384 | tf_op jit(solution)/shard_map/all_to_all | solution.py:120
  276.4 109.7 %all-to-all-start.8 = ((f32[8,1,256]{2,1,0:T(1,128)}), f32[8,1,256]{2,1,0:T(1,128)S(1)}, u32[]{:S(2)}, u32[]{:S(2)}) async-start(f32[8,1,256]{2,1,0:T(1,128)} %broadcast_select_fusion), calls=%async_computation.8 | async-start | bytes 16384 | tf_op jit(solution)/shard_map/all_to_all | solution.py:127
  288.6 46.1 %copy-start.13 = (bf16[128,1024]{1,0:T(8,128)(2,1)S(1)}, bf16[128,1024]{1,0:T(8,128)(2,1)}, u32[]{:S(2)}) copy-start(bf16[128,1024]{1,0:T(8,128)(2,1)} %convolution_convert_fusion.4) | copy-start | bytes 786436
  334.7 48.1 %copy-start.2 = (bf16[1,128,4,256]{1,3,2,0:T(8,128)(2,1)S(1)}, bf16[1,128,4,256]{1,3,2,0:T(8,128)(2,1)}, u32[]{:S(2)}) copy-start(bf16[1,128,4,256]{1,3,2,0:T(8,128)(2,1)} %get-tuple-element.21) | copy-start | bytes 786436
  385.2 8.2 %copy-start.10 = (bf16[128,1024]{1,0:T(8,128)(2,1)S(1)}, bf16[128,1024]{1,0:T(8,128)(2,1)}, u32[]{:S(2)}) copy-start(bf16[128,1024]{1,0:T(8,128)(2,1)} %get-tuple-element.34) | copy-start | bytes 786436
  386.2 9.7 %copy-start.11 = (bf16[128,1024]{1,0:T(8,128)(2,1)S(1)}, bf16[128,1024]{1,0:T(8,128)(2,1)}, u32[]{:S(2)}) copy-start(bf16[128,1024]{1,0:T(8,128)(2,1)} %get-tuple-element.36) | copy-start | bytes 786436
  386.2 15.2 %all-to-all-start.5 = ((bf16[3,4,128,256]{3,2,0,1:T(8,128)(2,1)}), bf16[3,4,128,256]{3,2,0,1:T(8,128)(2,1)S(1)}, u32[]{:S(2)}, u32[]{:S(2)}) async-start(bf16[3,4,128,256]{3,2,0,1:T(8,128)(2,1)} %maximum_bitcast_fusion.1), calls=%async_computation.5 | async-start | bytes 1572864 | tf_op jit(solution)/shard_map/all_to_all | solution.py:27
  401.4 15.9 %all-to-all-start.3 = ((bf16[3,4,128,256]{3,2,0,1:T(8,128)(2,1)}), bf16[3,4,128,256]{3,2,0,1:T(8,128)(2,1)}, u32[]{:S(2)}, u32[]{:S(2)}) async-start(bf16[3,4,128,256]{3,2,0,1:T(8,128)(2,1)} %maximum_bitcast_fusion), calls=%async_computation.3 | async-start | bytes 1572864 | tf_op jit(solution)/shard_map/all_to_all | solution.py:27
  417.3 17.9 %all-to-all-start.6 = ((bf16[8,128,256]{2,1,0:T(8,128)(2,1)}), bf16[8,128,256]{2,1,0:T(8,128)(2,1)S(1)}, u32[]{:S(2)}, u32[]{:S(2)}) async-start(bf16[8,128,256]{2,1,0:T(8,128)(2,1)} %select_select_fusion), calls=%async_computation.6 | async-start | bytes 1048576 | tf_op jit(solution)/shard_map/all_to_all | solution.py:116
  420.8 1.5 copy-start.5
  420.8 1.5 copy-start.7
  420.8 1.6 copy-start.8
  420.8 1.7 copy-start.9
Sparse Core Ops, SparseCore 0:
  82.3 48.3 all-gather.8
  133.3 48.5 all-gather.10
  184.5 48.5 all-gather.6
  235.6 47.4 all-gather.14
  285.0 47.5 all-gather.12
  335.2 47.6 all-gather.16
